TPU v7x, 32 devices: a whole 2x2x4 slice. The times are simulated.
32 devices in a mesh: row: 8 (over z, y), col: 4 (over x, core).
Axes of the slice: x: 2, y: 2, z: 4, core: 2. Of those that a mesh axis runs over, the one named last changes fastest.
Arguments:
- embeddings: bfloat16 [512, 1024], P(('row', 'col')), may hold values from -20 to 20
- group_ids: int32 [512], P(('row', 'col')), may hold values from 0 to 127, as said below
Outputs:
- loss: float32 [], replicated
- grad: bfloat16 [512, 1024], P(('row', 'col'))
Inputs may be any that keep to these rules, and one draw needn't show every extreme that they name: `group_ids`: every group id is held by exactly 4 rows, spread over the batch.
All inputs are finite; a program needn't handle non-finite values.
Results may differ from a plain program's by a relative error of at most 0.0045.
Values may be sent and summed in bfloat16 or wider, within the bound.
No kernel may reach another device: no remote copies, remote signals or barrier semaphores. Data moves between devices by JAX's collectives and lax.ppermute only.
A program may use at most 64 MiB of HBM per device.

v0:
```python
import jax
import jax.numpy as jnp
from jax import lax
from jax.sharding import PartitionSpec as P


def joined(part, axis, combine):
    gathered = jax.tree.map(lambda a: lax.all_gather(a, axis), part)

    def take(source):
        return jax.tree.map(lambda a: lax.dynamic_index_in_dim(a, source, 0, False), gathered)

    return lax.fori_loop(
        1, lax.axis_size(axis), lambda source, state: combine(state, take(source)), take(0)
    )


def combine_stats(first, second):
    peak = jnp.maximum(first[0], second[0])
    total = first[1] * jnp.exp(first[0] - peak) + second[1] * jnp.exp(second[0] - peak)
    return (peak, total, first[2] + second[2], first[3] + second[3])


def on_device(embeddings, group_ids):
    row_count = lax.axis_size("row")
    col_count = lax.axis_size("col")
    row_index = lax.axis_index("row")
    col_index = lax.axis_index("col")
    rows = embeddings.shape[0]
    width = embeddings.shape[1]
    scale = 1.0 / jnp.sqrt(jnp.float32(width))
    whole = rows * row_count * col_count
    queries, query_groups = (
        lax.all_gather(embeddings, "col", axis=0, tiled=True),
        lax.all_gather(group_ids, "col", axis=0, tiled=True),
    )
    keys, key_groups = (
        lax.all_gather(embeddings, "row", axis=0, tiled=True),
        lax.all_gather(group_ids, "row", axis=0, tiled=True),
    )
    query_len = rows * col_count
    key_len = rows * row_count
    query_pos = row_index * query_len + jnp.arange(query_len, dtype=jnp.int32)
    key_local = jnp.arange(key_len, dtype=jnp.int32)
    key_pos = (key_local // rows * col_count + col_index) * rows + key_local % rows
    scores = (
        lax.dot_general(queries, keys, (((1,), (1,)), ((), ())), preferred_element_type=jnp.float32)
        * scale
    )
    selfs = query_pos[:, None] == key_pos[None, :]
    positive = jnp.logical_and(query_groups[:, None] == key_groups[None, :], jnp.logical_not(selfs))
    masked = jnp.where(selfs, jnp.float32(-1e30), scores)
    peak = jnp.max(masked, axis=1)
    total = jnp.sum(jnp.exp(masked - peak[:, None]), axis=1)
    possum = jnp.sum(jnp.where(positive, scores, jnp.float32(0.0)), axis=1)
    count = jnp.sum(positive.astype(jnp.float32), axis=1)
    peak, total, possum, count = joined((peak, total, possum, count), "col", combine_stats)
    lse = peak + jnp.log(total)
    inverse = 1.0 / count
    row_loss = lse - possum * inverse
    own_start = col_index * rows
    own_loss = lax.dynamic_slice_in_dim(row_loss, own_start, rows, 0)
    loss = lax.psum(jnp.sum(own_loss), ("row", "col")) / whole
    weight = (
        jnp.exp(masked - lse[:, None]) - jnp.where(positive, inverse[:, None], jnp.float32(0.0))
    ) / whole
    weight = weight.astype(jnp.bfloat16)
    own_lse = lax.dynamic_slice_in_dim(lse, own_start, rows, 0)
    own_inverse = lax.dynamic_slice_in_dim(inverse, own_start, rows, 0)
    key_lse, key_inverse = (
        lax.all_gather(own_lse, "row", axis=0, tiled=True),
        lax.all_gather(own_inverse, "row", axis=0, tiled=True),
    )
    mirrored = (
        jnp.exp(masked - key_lse[None, :])
        - jnp.where(positive, key_inverse[None, :], jnp.float32(0.0))
    ) / whole
    mirrored = mirrored.astype(jnp.bfloat16)
    both_term = jnp.dot(weight, keys, preferred_element_type=jnp.float32) + jnp.dot(
        mirrored, keys, preferred_element_type=jnp.float32
    )
    grad = scale * lax.psum_scatter(both_term, "col", scatter_dimension=0, tiled=True)
    return (loss, grad.astype(jnp.bfloat16))


def solution(mesh):
    in_specs = (P(("row", "col"), None), P(("row", "col")))
    out_specs = (P(), P(("row", "col"), None))
    return jax.shard_map(
        on_device, mesh=mesh, in_specs=in_specs, out_specs=out_specs, check_vma=False
    )
```

profile of v0, /device:TPU:12, one launch (start us, length us, event | category | flops | bytes accessed | tf_op | source)
XLA Modules:
  0.0 142.9 jit_solution(13007018784665534406)
XLA Ops:
  7.2 5.6 %all_gather.42 = bf16[64,1024]{1,0:T(8,128)(2,1)S(1)} all-gather(bf16[16,1024]{1,0:T(8,128)(2,1)} %param.4), channel_id=1, replica_groups=mesh['row'=8,'col'=4] {'col'}, dimensions={0}, use_global_device_ids=true | all-gather | bytes 163840 | tf_op jit(solution)/shard_map/all_gather | solution.py:34
  12.9 28.3 %all_gather.43 = bf16[128,1024]{1,0:T(8,128)(2,1)S(1)} all-gather(bf16[16,1024]{1,0:T(8,128)(2,1)S(1)} %copy-done), channel_id=1, replica_groups=mesh['row'=8,'col'=4] {'row'}, dimensions={0}, use_global_device_ids=true | all-gather | bytes 294912 | tf_op jit(solution)/shard_map/all_gather | solution.py:38
  41.1 0.6 copy-done.3
  41.8 0.7 dynamic-slice.3
  42.4 0.6 dynamic-slice
  45.0 0.6 copy-done.1
  45.7 0.2 dynamic-update-slice.2
  45.9 4.9 %all-reduce.2 = s32[64]{0:T(128)S(1)} all-reduce(s32[64]{0:T(128)S(1)} %dynamic-update-slice.2), channel_id=1, replica_groups=mesh['row'=8,'col'=4] {'col'}, use_global_device_ids=true, to_apply=%add.2 | all-reduce | flops 64 | bytes 512
  50.8 0.2 dynamic-update-slice.3
  51.0 11.3 %all-reduce.3 = s32[128]{0:T(128)S(1)} all-reduce(s32[128]{0:T(128)S(1)} %dynamic-update-slice.3), channel_id=1, replica_groups=mesh['row'=8,'col'=4] {'row'}, use_global_device_ids=true, to_apply=%add.3 | all-reduce | flops 128 | bytes 1024
  62.2 0.3 fusion.10
  62.5 0.2 dynamic-update-slice
  62.8 0.2 select_reduce_fusion
  63.0 0.2 dynamic-update-slice.5
  63.3 0.2 dynamic-update-slice.4
  63.5 0.2 dynamic-update-slice.1
  63.7 5.6 %all-reduce.9 = (f32[256]{0:T(256)S(1)}, f32[256]{0:T(256)S(1)}, f32[256]{0:T(256)S(1)}, f32[256]{0:T(256)S(1)}) all-reduce(f32[256]{0:T(256)S(1)} %dynamic-update-slice, f32[256]{0:T(256)S(1)} %dynamic-update-slice.1, f32[256]{0:T(256)S(1)} %dynamic-update-slice.4, f32[256]{0:T(256)S(1)} %dynamic-update-slice.5), channel_id=2, replica_groups=mesh['row'=8,'col'=4] {'col'}, use_global_device_ids=true, to_apply=%add | all-reduce | flops 1024 | bytes 8192
  69.8 0.2 fusion.11
  70.1 0.2 dynamic-slice_dynamic-update-slice_fusion
  70.4 17.1 %all-reduce.8 = (f32[128]{0:T(128)S(1)}, f32[128]{0:T(128)S(1)}) all-reduce(f32[128]{0:T(128)S(1)} %dynamic-slice_dynamic-update-slice_fusion, f32[128]{0:T(128)S(1)} %dynamic-slice_dynamic-update-slice_fusion.1), channel_id=1, replica_groups=mesh['row'=8,'col'=4] {'row'}, use_global_device_ids=true, to_apply=%add.7 | all-reduce | flops 256 | bytes 2048
  87.5 0.9 convolution_add_fusion
  88.5 0.7 dynamic-slice_reduce_fusion
  89.2 43.6 %psum.7 = f32[]{:T(128)} all-reduce(f32[]{:T(128)} %dynamic-slice_reduce_fusion), channel_id=1, replica_groups=mesh['row'=8,'col'=4] {'row','col'}, use_global_device_ids=true, to_apply=%region_7.8 | all-reduce | flops 1 | bytes 8 | tf_op jit(solution)/shard_map/psum | solution.py:63
  133.5 1.5 %multiply_convert_fusion = bf16[16,1024]{1,0:T(8,128)(2,1)} fusion(f32[16,1024]{1,0:T(8,128)} %reduce-scatter.2.cloned.1.call-done), kind=kLoop, calls=%fused_computation.15 | loop fusion | flops 32768 | bytes 98304 | tf_op jit(solution)/shard_map/convert_element_type | solution.py:83
  (36 shorter events, 0.9 us)
Async XLA Ops:
  7.2 126.3 %reduce-scatter.2.cloned.1.call-start = ((), (), s32[]{:S(2)}) async-start(), calls=%async_computation.1 | async-start | bytes 327680 | tf_op jit(solution)/shard_map/reduce_scatter | solution.py:82
  7.2 5.6 %copy-start = (bf16[16,1024]{1,0:T(8,128)(2,1)S(1)}, bf16[16,1024]{1,0:T(8,128)(2,1)}, u32[]{:S(2)}) copy-start(bf16[16,1024]{1,0:T(8,128)(2,1)} %param.4) | copy-start | bytes 98308
  41.1 0.7 copy-start.3
  41.8 0.7 copy-start.2
  45.0 0.7 copy-start.1
Sparse Core Ops, SparseCore 0:
  88.6 20.8 reduce-scatter.1
where the time goes:
time: 143 us
  blocking collectives  116 us (81%)
  between operations  17.9 us (13%)
  local copies, waits for them, and re-layouts  4.48 us (3%)
  other arithmetic  2.51 us (2%)
  matrix products  1.48 us (1%)
    psum x1, blocking collectives, on_device(): loss = lax.psum(jnp.sum(own_loss), ('row', 'col')) / whole  43.6 us
    unnamed x4, blocking collectives  38.9 us
    all_gather x1, blocking collectives, on_device(): lax.all_gather(embeddings, 'row', axis=0, tiled=True)  28.3 us
    all_gather x1, blocking collectives, on_device(): lax.all_gather(embeddings, 'col', axis=0, tiled=True)  5.63 us
    unnamed x25, local copies, waits for them, and re-layouts  4.14 us
  transfers between devices with their start and end apart: 1, of which 0 were waited for; matrix products, arithmetic and copies ran while one was open for 0% of the time, Pallas kernels for 0%

commit v1 on v0

--- a/solution.py
+++ b/solution.py
@@ -1,7 +1,17 @@
+import functools
 import jax
 import jax.numpy as jnp
 from jax import lax
 from jax.sharding import PartitionSpec as P
+
+
+def place_the_entries(xin, group_axis):
+    lower = jnp.stack([xin for _ in range(lax.axis_size(group_axis))], axis=0)
+    carry = lax.all_to_all(lower, group_axis, split_axis=0, concat_axis=0)
+    return jnp.concatenate(carry, axis=0)
+
+
+_connect_object = functools.partial(place_the_entries, group_axis="row")
 
 
 def joined(part, axis, combine):
@@ -35,7 +45,7 @@
         lax.all_gather(group_ids, "col", axis=0, tiled=True),
     )
     keys, key_groups = (
-        lax.all_gather(embeddings, "row", axis=0, tiled=True),
+        _connect_object(embeddings),
         lax.all_gather(group_ids, "row", axis=0, tiled=True),
     )
     query_len = rows * col_count

time: 143 us -> 120 us (0.84)
  blocking collectives: 116 us -> 86 us
  starting transfers between devices: 0.04 us -> 6.36 us
    all_gather x1 -> x0, blocking collectives: 28.3 us -> none  [on_device(): lax.all_gather(embeddings, 'row', axis=0, tiled=True)]
    all_to_all x0 -> x1, starting transfers between devices: none -> 6.35 us  [place_the_entries(): carry = lax.all_to_all(lower, group_axis, split_axis=0, concat_axis=0)]
    another operation x0 -> x1, local copies, waits for them, and re-layouts: none -> 1.48 us  [place_the_entries(): lower = jnp.stack([xin for _ in range(lax.axis_size(group_axis))], axis=0)]
  transfers between devices with their start and end apart: 1 -> 2, of which waited for: 0 -> 0; matrix products, arithmetic and copies ran while one was open for 0% -> 2% of each run, Pallas kernels for 0% -> 0%
where the time goes in v1:
time: 120 us
  blocking collectives  86 us (72%)
  between operations  17.8 us (15%)
  starting transfers between devices  6.36 us (5%)
  local copies, waits for them, and re-layouts  5.32 us (4%)
  other arithmetic  2.51 us (2%)
  matrix products  1.48 us (1%)
    psum x1, blocking collectives, on_device(): loss = lax.psum(jnp.sum(own_loss), ('row', 'col')) / whole  43 us
    unnamed x4, blocking collectives  37.6 us
    all_to_all x1, starting transfers between devices, place_the_entries(): carry = lax.all_to_all(lower, group_axis, split_axis=0, concat_axis=0)  6.35 us
    all_gather x1, blocking collectives, on_device(): lax.all_gather(embeddings, 'col', axis=0, tiled=True)  5.4 us
    unnamed x25, local copies, waits for them, and re-layouts  3.5 us
  transfers between devices with their start and end apart: 2, of which 0 were waited for; matrix products, arithmetic and copies ran while one was open for 2% of the time, Pallas kernels for 0%

profile of v1, /device:TPU:12, one launch (start us, length us, event | category | flops | bytes accessed | tf_op | source)
XLA Modules:
  0.0 119.6 jit_solution(8249292524868331445)
XLA Ops:
  7.2 1.5 %stack.2 = bf16[8,16,1024]{2,1,0:T(8,128)(2,1)} broadcast(bf16[16,1024]{1,0:T(8,128)(2,1)} %param.4), dimensions={1,2} | broadcast | bytes 294912 | tf_op jit(solution)/shard_map/stack | solution.py:9
  8.6 6.4 %all-to-all-start = ((bf16[8,16,1024]{2,1,0:T(8,128)(2,1)}), bf16[8,16,1024]{2,1,0:T(8,128)(2,1)S(1)}, u32[]{:S(2)}, u32[]{:S(2)}) async-start(bf16[8,16,1024]{2,1,0:T(8,128)(2,1)} %stack.2), calls=%async_computation | async-start | bytes 524288 | tf_op jit(solution)/shard_map/all_to_all | solution.py:10
  15.0 0.6 dynamic-slice.3
  15.7 0.6 dynamic-slice
  18.2 0.6 copy-done.1
  18.8 0.2 dynamic-update-slice.3
  19.0 0.2 dynamic-update-slice.2
  19.2 10.4 %all-reduce.3 = s32[128]{0:T(128)S(1)} all-reduce(s32[128]{0:T(128)S(1)} %dynamic-update-slice.3), channel_id=1, replica_groups=mesh['row'=8,'col'=4] {'row'}, use_global_device_ids=true, to_apply=%add.3 | all-reduce | flops 128 | bytes 1024
  29.6 4.9 %all-reduce.2 = s32[64]{0:T(128)S(1)} all-reduce(s32[64]{0:T(128)S(1)} %dynamic-update-slice.2), channel_id=1, replica_groups=mesh['row'=8,'col'=4] {'col'}, use_global_device_ids=true, to_apply=%add.2 | all-reduce | flops 64 | bytes 512
  34.5 5.4 %all_gather.39 = bf16[64,1024]{1,0:T(8,128)(2,1)S(1)} all-gather(bf16[16,1024]{1,0:T(8,128)(2,1)S(1)} %copy-done), channel_id=1, replica_groups=mesh['row'=8,'col'=4] {'col'}, dimensions={0}, use_global_device_ids=true | all-gather | bytes 163840 | tf_op jit(solution)/shard_map/all_gather | solution.py:44
  39.9 0.3 fusion.10
  40.2 0.2 dynamic-update-slice
  40.5 0.2 select_reduce_fusion
  40.7 0.2 dynamic-update-slice.5
  40.9 0.2 dynamic-update-slice.4
  41.2 0.2 dynamic-update-slice.1
  41.4 6.4 %all-reduce.9 = (f32[256]{0:T(256)S(1)}, f32[256]{0:T(256)S(1)}, f32[256]{0:T(256)S(1)}, f32[256]{0:T(256)S(1)}) all-reduce(f32[256]{0:T(256)S(1)} %dynamic-update-slice, f32[256]{0:T(256)S(1)} %dynamic-update-slice.1, f32[256]{0:T(256)S(1)} %dynamic-update-slice.4, f32[256]{0:T(256)S(1)} %dynamic-update-slice.5), channel_id=2, replica_groups=mesh['row'=8,'col'=4] {'col'}, use_global_device_ids=true, to_apply=%add | all-reduce | flops 1024 | bytes 8192
  48.3 0.2 fusion.11
  48.6 0.2 dynamic-slice_dynamic-update-slice_fusion
  48.9 15.9 %all-reduce.8 = (f32[128]{0:T(128)S(1)}, f32[128]{0:T(128)S(1)}) all-reduce(f32[128]{0:T(128)S(1)} %dynamic-slice_dynamic-update-slice_fusion, f32[128]{0:T(128)S(1)} %dynamic-slice_dynamic-update-slice_fusion.1), channel_id=1, replica_groups=mesh['row'=8,'col'=4] {'row'}, use_global_device_ids=true, to_apply=%add.7 | all-reduce | flops 256 | bytes 2048
  64.8 0.9 convolution_add_fusion
  65.8 0.7 dynamic-slice_reduce_fusion
  66.4 43.0 %psum.7 = f32[]{:T(128)} all-reduce(f32[]{:T(128)} %dynamic-slice_reduce_fusion), channel_id=1, replica_groups=mesh['row'=8,'col'=4] {'row','col'}, use_global_device_ids=true, to_apply=%region_7.8 | all-reduce | flops 1 | bytes 8 | tf_op jit(solution)/shard_map/psum | solution.py:73
  110.2 1.5 %multiply_convert_fusion = bf16[16,1024]{1,0:T(8,128)(2,1)} fusion(f32[16,1024]{1,0:T(8,128)} %reduce-scatter.2.cloned.1.call-done), kind=kLoop, calls=%fused_computation.15 | loop fusion | flops 32768 | bytes 98304 | tf_op jit(solution)/shard_map/convert_element_type | solution.py:93
  (38 shorter events, 0.9 us)
Async XLA Ops:
  8.6 6.4 %copy-start.3 = (u32[32]{0:T(128)S(1)}, u32[32]{0:T(128)}, u32[]{:S(2)}) copy-start(u32[32]{0:T(128)} %constant.134) | copy-start | bytes 388
  8.6 7.0 %copy-start.2 = (u32[32]{0:T(128)S(1)}, u32[32]{0:T(128)}, u32[]{:S(2)}) copy-start(u32[32]{0:T(128)} %constant.119) | copy-start | bytes 388
  8.6 31.3 %all-to-all-start = ((bf16[8,16,1024]{2,1,0:T(8,128)(2,1)}), bf16[8,16,1024]{2,1,0:T(8,128)(2,1)S(1)}, u32[]{:S(2)}, u32[]{:S(2)}) async-start(bf16[8,16,1024]{2,1,0:T(8,128)(2,1)} %stack.2), calls=%async_computation | async-start | bytes 524288 | tf_op jit(solution)/shard_map/all_to_all | solution.py:10
  15.0 19.5 %copy-start = (bf16[16,1024]{1,0:T(8,128)(2,1)S(1)}, bf16[16,1024]{1,0:T(8,128)(2,1)}, u32[]{:S(2)}) copy-start(bf16[16,1024]{1,0:T(8,128)(2,1)} %param.4) | copy-start | bytes 98308
  15.0 95.1 %reduce-scatter.2.cloned.1.call-start = ((), (), s32[]{:S(2)}) async-start(), calls=%async_computation.2 | async-start | bytes 327680 | tf_op jit(solution)/shard_map/reduce_scatter | solution.py:92
  18.2 0.7 copy-start.1
Sparse Core Ops, SparseCore 0:
  65.9 20.6 reduce-scatter.1
